TPU v7x, 32 devices: a whole 2x2x4 slice. The times are simulated.
32 devices in a mesh: slab: 2 (over y), tile: 4 (over z), view: 4 (over x, core).
Axes of the slice: x: 2, y: 2, z: 4, core: 2. Of those that a mesh axis runs over, the one named last changes fastest.
Arguments:
- recorded: float32 [4, 96, 32, 1024], P('view', 'tile', 'slab'), parts along dimension 2, may hold values from 0.5 to 2
- psf_taps: float32 [4, 3, 15], P('view'), may hold values from 0.2 to 1
- estimate: float32 [96, 32, 1024], P('tile', 'slab'), parts along dimension 1, may hold values from 0.5 to 2
Outputs:
- joined: float32 [96, 32, 1024], P('tile', 'slab'), parts along dimension 1
There are 2 independent parts, one for each index of `slab`. A program takes and returns all parts, laid end to end along the dimension named above; an argument that names none is the same for every part. Nothing has to cross between parts.
All inputs are finite; a program needn't handle non-finite values.
Results may differ from a plain program's by a relative error of at most 0.00002.
Values sent between devices are 32-bit elements; how exact they have to be, the bound alone decides.
No kernel may reach another device: no remote copies, remote signals or barrier semaphores. Data moves between devices by JAX's collectives and lax.ppermute only.
A program may use at most 64 MiB of HBM per device.

v0:
```python
import jax
import jax.numpy as jnp
from jax import lax
from jax.sharding import PartitionSpec as P

RADIUS = 7
ITERS = 2


def with_halo(shard, sides, width):
    for axis, dim in sides:
        devices, length = (lax.axis_size(axis), shard.shape[dim])
        up = [(i, (i + 1) % devices) for i in range(devices - 1)]
        down = [(j, i) for i, j in up]
        last = lax.slice_in_dim(shard, length - width, length, axis=dim)
        initial = lax.slice_in_dim(shard, 0, width, axis=dim)
        before = lax.ppermute(last, axis, up)
        after = lax.ppermute(initial, axis, down)
        shard = jnp.concatenate([before, shard, after], axis=dim)
    return shard


def valid_along(padded, kernel_row, axis_num, mirrored):
    length_out = padded.shape[axis_num] - 2 * RADIUS
    summed = jnp.zeros(
        padded.shape[:axis_num] + (length_out,) + padded.shape[axis_num + 1 :], jnp.float32
    )
    for offset in range(2 * RADIUS + 1):
        weight = kernel_row[2 * RADIUS - offset] if mirrored else kernel_row[offset]
        summed = summed + weight * lax.slice_in_dim(
            padded, offset, offset + length_out, axis=axis_num
        )
    return summed


def along(values_in, kernel_row, axis_num, mirrored):
    widths = [(0, 0)] * values_in.ndim
    widths[axis_num] = (RADIUS, RADIUS)
    return valid_along(jnp.pad(values_in, widths), kernel_row, axis_num, mirrored)


def finish_zy(values_in, kernel_view, mirrored):
    result = along(values_in, kernel_view[1], 1, mirrored)
    return along(result, kernel_view[2], 2, mirrored)


def local(recorded, psf_taps, estimate):
    kernel = psf_taps / jnp.sum(psf_taps, axis=2, keepdims=True)
    local_views = recorded.shape[0]
    view_total = lax.axis_size("view") * local_views
    for iteration in range(ITERS):
        extended = with_halo(estimate, (("tile", 0),), RADIUS)
        kernel_view = kernel[0]
        blurred = finish_zy(valid_along(extended, kernel_view[0], 0, False), kernel_view, False)
        quotient = recorded[0] / blurred
        quotient_wide = with_halo(quotient, (("tile", 0),), RADIUS)
        correction = finish_zy(
            valid_along(quotient_wide, kernel_view[0], 0, True), kernel_view, True
        )
        log_terms = jnp.log(correction)
        log_total = lax.psum(log_terms, "view")
        estimate = estimate * jnp.exp(log_total / view_total)
    return estimate


def solution(mesh):
    in_specs = (P("view", "tile", "slab", None), P("view", None, None), P("tile", "slab", None))
    out_specs = P("tile", "slab", None)
    return jax.shard_map(local, mesh=mesh, in_specs=in_specs, out_specs=out_specs, check_vma=False)
```

profile of v0, /device:TPU:0, one launch (start us, length us, event | category | flops | bytes accessed | tf_op | source)
XLA Modules:
  0.0 333.5 jit_solution(3361568924771776846)
XLA Ops:
  6.5 1.3 fusion.365
  7.9 5.0 %collective-permute-start = (f32[7,16,1024]{2,1,0:T(8,128)S(1)}, f32[7,16,1024]{2,1,0:T(8,128)S(1)}, u32[]{:S(2)}, u32[]{:S(2)}) collective-permute-start(f32[7,16,1024]{2,1,0:T(8,128)S(1)} %get-tuple-element.13), channel_id=1, source_target_pairs={{0,4},{4,8},{8,12},{1,5},{5,9},{9,13},{2,6},{6,10},{10,14},{3,7},{... | collective-permute-start | bytes 1376264 | tf_op jit(solution)/shard_map/ppermute | solution.py:17
  12.9 1.3 collective-permute-start.1
  16.5 6.1 %collective-permute-done = f32[7,16,1024]{2,1,0:T(8,128)S(1)} collective-permute-done((f32[7,16,1024]{2,1,0:T(8,128)S(1)}, f32[7,16,1024]{2,1,0:T(8,128)S(1)}, u32[]{:S(2)}, u32[]{:S(2)}) %collective-permute-start) | collective-permute-done | bytes 458784 | tf_op jit(solution)/shard_map/ppermute | solution.py:17
  23.0 3.7 %collective-permute-done.1 = f32[7,16,1024]{2,1,0:T(8,128)S(1)} collective-permute-done((f32[7,16,1024]{2,1,0:T(8,128)S(1)}, f32[7,16,1024]{2,1,0:T(8,128)S(1)}, u32[]{:S(2)}, u32[]{:S(2)}) %collective-permute-start.1) | collective-permute-done | bytes 458784 | tf_op jit(solution)/shard_map/ppermute | solution.py:18
  26.8 12.1 %fusion.346 = f32[24,16,1024]{2,1,0:T(8,128)S(1)} fusion(f32[31,16,1024]{2,1,0:T(8,128)S(1)} %constant_dynamic-update-slice_fusion.2, f32[31,16,1024]{2,1,0:T(8,128)S(1)} %get-tuple-element.11, f32[24,16,1024]{2,1,0:T(8,128)S(1)} %copy-done, f32[]{:T(128)} %bitcast.19, f32[]{:T(128)} %bitcast.18, f32[]{:T(128)} %bitcast.17, f32[]{:T(128)} %bitcast.16, ...), kind=kLoop, calls=%fused_computation.537 | loop fusion | flops 11403264 | bytes 25165884 | tf_op jit(solution)/shard_map/add | solution.py:30
  38.9 12.4 %fusion.242 = f32[24,16,1024]{2,1,0:T(8,128)S(1)} fusion(f32[24,16,1024]{2,1,0:T(8,128)S(1)} %fusion.346, f32[]{:T(128)} %bitcast.32, f32[]{:T(128)} %bitcast.31, f32[]{:T(128)} %bitcast.30, f32[]{:T(128)} %bitcast.29, f32[]{:T(128)} %bitcast.28, f32[]{:T(128)} %bitcast.27, f32[]{:T(128)} %bitcast.26, f32[]{:T(128)} %bitcast.25, f32[]{:T(128)} %bitcast.24, ...), kind=kLoop, calls=%fused_computation.426 | loop fusion | flops 11403264 | bytes 3145788 | tf_op jit(solution)/shard_map/add | solution.py:30
  51.2 15.3 %fusion.15 = f32[24,16,1024]{2,1,0:T(8,128)S(1)} fusion(f32[24,16,1024]{2,1,0:T(8,128)S(1)} %fusion.242, f32[1,24,16,1024]{3,2,1,0:T(8,128)S(1)} %copy-done.1, f32[]{:T(128)} %bitcast.45, f32[]{:T(128)} %bitcast.44, f32[]{:T(128)} %bitcast.43, f32[]{:T(128)} %bitcast.42, f32[]{:T(128)} %bitcast.41, f32[]{:T(128)} %bitcast.40, f32[]{:T(128)} %bitcast.39, ...), kind=kLoop, calls=%fused_computation.199 | loop fusion | flops 11796480 | bytes 4718652 | tf_op jit(solution)/shard_map/div | solution.py:55
  66.7 1.3 collective-permute-start.3
  68.0 4.8 %collective-permute-start.2 = (f32[7,16,1024]{2,1,0:T(8,128)S(1)}, f32[7,16,1024]{2,1,0:T(8,128)S(1)}, u32[]{:S(2)}, u32[]{:S(2)}) collective-permute-start(f32[7,16,1024]{2,1,0:T(8,128)S(1)} %get-tuple-element.9), channel_id=1, source_target_pairs={{0,4},{4,8},{8,12},{1,5},{5,9},{9,13},{2,6},{6,10},{10,14},{3,7},{... | collective-permute-start | bytes 1376264 | tf_op jit(solution)/shard_map/ppermute | solution.py:17
  72.7 7.0 %collective-permute-done.3 = f32[7,16,1024]{2,1,0:T(8,128)S(1)} collective-permute-done((f32[7,16,1024]{2,1,0:T(8,128)S(1)}, f32[7,16,1024]{2,1,0:T(8,128)S(1)}, u32[]{:S(2)}, u32[]{:S(2)}) %collective-permute-start.3) | collective-permute-done | bytes 458784 | tf_op jit(solution)/shard_map/ppermute | solution.py:18
  79.7 1.2 collective-permute-done.2
  80.9 12.3 %fusion.193 = f32[24,16,1024]{2,1,0:T(8,128)S(1)} fusion(f32[24,16,1024]{2,1,0:T(8,128)S(1)} %fusion.15, f32[7,16,1024]{2,1,0:T(8,128)S(1)} %collective-permute-done.3, f32[7,16,1024]{2,1,0:T(8,128)S(1)} %collective-permute-done.2, f32[]{:T(128)} %bitcast.19, f32[]{:T(128)} %bitcast.18, f32[]{:T(128)} %bitcast.17, f32[]{:T(128)} %bitcast.16, f32[]{:T(128)} %bitcast.15, ...), kind=kLoop, calls=%fused_computation.377 | loop fusion | flops 16908288 | bytes 4063292 | tf_op jit(solution)/shard_map/add | solution.py:30
  93.1 12.2 %fusion.270 = f32[24,16,1024]{2,1,0:T(8,128)S(1)} fusion(f32[24,16,1024]{2,1,0:T(8,128)S(1)} %fusion.193, f32[]{:T(128)} %bitcast.32, f32[]{:T(128)} %bitcast.31, f32[]{:T(128)} %bitcast.30, f32[]{:T(128)} %bitcast.29, f32[]{:T(128)} %bitcast.28, f32[]{:T(128)} %bitcast.27, f32[]{:T(128)} %bitcast.26, f32[]{:T(128)} %bitcast.25, f32[]{:T(128)} %bitcast.24, ...), kind=kLoop, calls=%fused_computation.454 | loop fusion | flops 11403264 | bytes 3145788 | tf_op jit(solution)/shard_map/add | solution.py:30
  105.4 16.2 %fusion.361 = f32[24,16,1024]{2,1,0:T(8,128)} fusion(f32[24,16,1024]{2,1,0:T(8,128)S(1)} %fusion.270, f32[]{:T(128)} %bitcast.45, f32[]{:T(128)} %bitcast.44, f32[]{:T(128)} %bitcast.43, f32[]{:T(128)} %bitcast.42, f32[]{:T(128)} %bitcast.41, f32[]{:T(128)} %bitcast.40, f32[]{:T(128)} %bitcast.39, f32[]{:T(128)} %bitcast.38, f32[]{:T(128)} %bitcast.37, ...), kind=kLoop, calls=%fused_computation.567 | loop fusion | flops 11403264 | bytes 3145788 | tf_op jit(solution)/shard_map/log | solution.py:60
  121.7 45.1 %all-reduce.11.cloned.1.call-done = f32[24,16,1024]{2,1,0:T(8,128)} async-done(((f32[24,16,1024]{2,1,0:T(8,128)}), f32[24,16,1024]{2,1,0:T(8,128)}) %all-reduce.11.cloned.1.call-update) | async-done | bytes 1572880 | tf_op jit(solution)/shard_map/psum | solution.py:61
  166.8 1.7 exponential_multiply_fusion.1
  168.5 1.3 collective-permute-start.5
  169.8 4.6 %collective-permute-start.4 = (f32[7,16,1024]{2,1,0:T(8,128)S(1)}, f32[7,16,1024]{2,1,0:T(8,128)S(1)}, u32[]{:S(2)}, u32[]{:S(2)}) collective-permute-start(f32[7,16,1024]{2,1,0:T(8,128)S(1)} %get-tuple-element.7), channel_id=1, source_target_pairs={{0,4},{4,8},{8,12},{1,5},{5,9},{9,13},{2,6},{6,10},{10,14},{3,7},{... | collective-permute-start | bytes 1376264 | tf_op jit(solution)/shard_map/ppermute | solution.py:17
  174.4 8.2 %collective-permute-done.5 = f32[7,16,1024]{2,1,0:T(8,128)S(1)} collective-permute-done((f32[7,16,1024]{2,1,0:T(8,128)S(1)}, f32[7,16,1024]{2,1,0:T(8,128)S(1)}, u32[]{:S(2)}, u32[]{:S(2)}) %collective-permute-start.5) | collective-permute-done | bytes 458784 | tf_op jit(solution)/shard_map/ppermute | solution.py:18
  183.8 12.2 %fusion.155 = f32[24,16,1024]{2,1,0:T(8,128)S(1)} fusion(f32[24,16,1024]{2,1,0:T(8,128)S(1)} %exponential_multiply_fusion.1, f32[7,16,1024]{2,1,0:T(8,128)S(1)} %collective-permute-done.5, f32[7,16,1024]{2,1,0:T(8,128)S(1)} %collective-permute-done.4, f32[]{:T(128)} %bitcast.19, f32[]{:T(128)} %bitcast.18, f32[]{:T(128)} %bitcast.17, f32[]{:T(128)} %bitcast.16, ...), kind=kLoop, calls=%fused_computation.339 | loop fusion | flops 16908288 | bytes 4063292 | tf_op jit(solution)/shard_map/add | solution.py:30
  195.9 12.4 %fusion.298 = f32[24,16,1024]{2,1,0:T(8,128)S(1)} fusion(f32[24,16,1024]{2,1,0:T(8,128)S(1)} %fusion.155, f32[]{:T(128)} %bitcast.32, f32[]{:T(128)} %bitcast.31, f32[]{:T(128)} %bitcast.30, f32[]{:T(128)} %bitcast.29, f32[]{:T(128)} %bitcast.28, f32[]{:T(128)} %bitcast.27, f32[]{:T(128)} %bitcast.26, f32[]{:T(128)} %bitcast.25, f32[]{:T(128)} %bitcast.24, ...), kind=kLoop, calls=%fused_computation.482 | loop fusion | flops 11403264 | bytes 3145788 | tf_op jit(solution)/shard_map/add | solution.py:30
  208.3 15.3 %fusion.72 = f32[24,16,1024]{2,1,0:T(8,128)S(1)} fusion(f32[24,16,1024]{2,1,0:T(8,128)S(1)} %fusion.298, f32[1,24,16,1024]{3,2,1,0:T(8,128)S(1)} %copy-done.2, f32[]{:T(128)} %bitcast.45, f32[]{:T(128)} %bitcast.44, f32[]{:T(128)} %bitcast.43, f32[]{:T(128)} %bitcast.42, f32[]{:T(128)} %bitcast.41, f32[]{:T(128)} %bitcast.40, f32[]{:T(128)} %bitcast.39, ...), kind=kLoop, calls=%fused_computation.256 | loop fusion | flops 11796480 | bytes 4718652 | tf_op jit(solution)/shard_map/div | solution.py:55
  223.7 1.5 collective-permute-start.7
  225.3 5.0 %collective-permute-start.6 = (f32[7,16,1024]{2,1,0:T(8,128)S(1)}, f32[7,16,1024]{2,1,0:T(8,128)S(1)}, u32[]{:S(2)}, u32[]{:S(2)}) collective-permute-start(f32[7,16,1024]{2,1,0:T(8,128)S(1)} %get-tuple-element.5), channel_id=1, source_target_pairs={{0,4},{4,8},{8,12},{1,5},{5,9},{9,13},{2,6},{6,10},{10,14},{3,7},{... | collective-permute-start | bytes 1376264 | tf_op jit(solution)/shard_map/ppermute | solution.py:17
  230.3 7.1 %collective-permute-done.7 = f32[7,16,1024]{2,1,0:T(8,128)S(1)} collective-permute-done((f32[7,16,1024]{2,1,0:T(8,128)S(1)}, f32[7,16,1024]{2,1,0:T(8,128)S(1)}, u32[]{:S(2)}, u32[]{:S(2)}) %collective-permute-start.7) | collective-permute-done | bytes 458784 | tf_op jit(solution)/shard_map/ppermute | solution.py:18
  237.4 1.4 collective-permute-done.6
  238.8 12.2 %fusion.117 = f32[24,16,1024]{2,1,0:T(8,128)S(1)} fusion(f32[24,16,1024]{2,1,0:T(8,128)S(1)} %fusion.72, f32[7,16,1024]{2,1,0:T(8,128)S(1)} %collective-permute-done.7, f32[7,16,1024]{2,1,0:T(8,128)S(1)} %collective-permute-done.6, f32[]{:T(128)} %bitcast.19, f32[]{:T(128)} %bitcast.18, f32[]{:T(128)} %bitcast.17, f32[]{:T(128)} %bitcast.16, f32[]{:T(128)} %bitcast.15, ...), kind=kLoop, calls=%fused_computation.301 | loop fusion | flops 16908288 | bytes 4063292 | tf_op jit(solution)/shard_map/add | solution.py:30
  251.0 12.2 %fusion.326 = f32[24,16,1024]{2,1,0:T(8,128)S(1)} fusion(f32[24,16,1024]{2,1,0:T(8,128)S(1)} %fusion.117, f32[]{:T(128)} %bitcast.32, f32[]{:T(128)} %bitcast.31, f32[]{:T(128)} %bitcast.30, f32[]{:T(128)} %bitcast.29, f32[]{:T(128)} %bitcast.28, f32[]{:T(128)} %bitcast.27, f32[]{:T(128)} %bitcast.26, f32[]{:T(128)} %bitcast.25, f32[]{:T(128)} %bitcast.24, ...), kind=kLoop, calls=%fused_computation.510 | loop fusion | flops 11403264 | bytes 3145788 | tf_op jit(solution)/shard_map/add | solution.py:30
  263.2 16.2 %fusion.360 = f32[24,16,1024]{2,1,0:T(8,128)} fusion(f32[24,16,1024]{2,1,0:T(8,128)S(1)} %fusion.326, f32[]{:T(128)} %bitcast.45, f32[]{:T(128)} %bitcast.44, f32[]{:T(128)} %bitcast.43, f32[]{:T(128)} %bitcast.42, f32[]{:T(128)} %bitcast.41, f32[]{:T(128)} %bitcast.40, f32[]{:T(128)} %bitcast.39, f32[]{:T(128)} %bitcast.38, f32[]{:T(128)} %bitcast.37, ...), kind=kLoop, calls=%fused_computation.566 | loop fusion | flops 11403264 | bytes 3145788 | tf_op jit(solution)/shard_map/log | solution.py:60
  279.4 44.4 %all-reduce.13.cloned.1.call-done = f32[24,16,1024]{2,1,0:T(8,128)} async-done(((f32[24,16,1024]{2,1,0:T(8,128)}), f32[24,16,1024]{2,1,0:T(8,128)}) %all-reduce.13.cloned.1.call-update) | async-done | bytes 1572880 | tf_op jit(solution)/shard_map/psum | solution.py:61
  323.8 2.8 exponential_multiply_fusion
  (24 shorter events, 4.2 us)
Async XLA Ops:
  6.5 16.1 %copy-start = (f32[24,16,1024]{2,1,0:T(8,128)S(1)}, f32[24,16,1024]{2,1,0:T(8,128)}, u32[]{:S(2)}) copy-start(f32[24,16,1024]{2,1,0:T(8,128)} %param.5) | copy-start | bytes 4718596
  6.5 7.7 %copy-start.3 = (f32[1,3,15]{2,0,1:T(1,128)S(1)}, f32[1,3,15]{2,0,1:T(1,128)}, u32[]{:S(2)}) copy-start(f32[1,3,15]{2,0,1:T(1,128)} %param.4) | copy-start | bytes 544
  6.5 160.2 %all-reduce.11.cloned.1.call-start = ((), (), s32[]{:S(2)}) async-start(), calls=%async_computation | async-start | bytes 3145728 | tf_op jit(solution)/shard_map/psum | solution.py:61
  7.9 14.7 %collective-permute-start = (f32[7,16,1024]{2,1,0:T(8,128)S(1)}, f32[7,16,1024]{2,1,0:T(8,128)S(1)}, u32[]{:S(2)}, u32[]{:S(2)}) collective-permute-start(f32[7,16,1024]{2,1,0:T(8,128)S(1)} %get-tuple-element.13), channel_id=1, source_target_pairs={{0,4},{4,8},{8,12},{1,5},{5,9},{9,13},{2,6},{6,10},{10,14},{3,7},{... | collective-permute-start | bytes 1376264 | tf_op jit(solution)/shard_map/ppermute | solution.py:17
  12.9 13.9 %collective-permute-start.1 = (f32[7,16,1024]{2,1,0:T(8,128)S(1)}, f32[7,16,1024]{2,1,0:T(8,128)S(1)}, u32[]{:S(2)}, u32[]{:S(2)}) collective-permute-start(f32[7,16,1024]{2,1,0:T(8,128)S(1)} %get-tuple-element.14), channel_id=1, source_target_pairs={{4,0},{8,4},{12,8},{5,1},{9,5},{13,9},{6,2},{10,6},{14,10},{7,3},{... | collective-permute-start | bytes 1376264 | tf_op jit(solution)/shard_map/ppermute | solution.py:18
  38.9 12.4 %copy-start.1 = (f32[1,24,16,1024]{3,2,1,0:T(8,128)S(1)}, f32[1,24,16,1024]{3,2,1,0:T(8,128)}, u32[]{:S(2)}) copy-start(f32[1,24,16,1024]{3,2,1,0:T(8,128)} %param.3) | copy-start | bytes 4718596
  66.7 13.0 %collective-permute-start.3 = (f32[7,16,1024]{2,1,0:T(8,128)S(1)}, f32[7,16,1024]{2,1,0:T(8,128)S(1)}, u32[]{:S(2)}, u32[]{:S(2)}) collective-permute-start(f32[7,16,1024]{2,1,0:T(8,128)S(1)} %get-tuple-element.10), channel_id=1, source_target_pairs={{4,0},{8,4},{12,8},{5,1},{9,5},{13,9},{6,2},{10,6},{14,10},{7,3},{... | collective-permute-start | bytes 1376264 | tf_op jit(solution)/shard_map/ppermute | solution.py:18
  68.0 12.9 %collective-permute-start.2 = (f32[7,16,1024]{2,1,0:T(8,128)S(1)}, f32[7,16,1024]{2,1,0:T(8,128)S(1)}, u32[]{:S(2)}, u32[]{:S(2)}) collective-permute-start(f32[7,16,1024]{2,1,0:T(8,128)S(1)} %get-tuple-element.9), channel_id=1, source_target_pairs={{0,4},{4,8},{8,12},{1,5},{5,9},{9,13},{2,6},{6,10},{10,14},{3,7},{... | collective-permute-start | bytes 1376264 | tf_op jit(solution)/shard_map/ppermute | solution.py:17
  121.6 202.2 %all-reduce.13.cloned.1.call-start = ((), (), s32[]{:S(2)}) async-start(), calls=%async_computation.1 | async-start | bytes 3145728 | tf_op jit(solution)/shard_map/psum | solution.py:61
  168.5 14.0 %collective-permute-start.5 = (f32[7,16,1024]{2,1,0:T(8,128)S(1)}, f32[7,16,1024]{2,1,0:T(8,128)S(1)}, u32[]{:S(2)}, u32[]{:S(2)}) collective-permute-start(f32[7,16,1024]{2,1,0:T(8,128)S(1)} %get-tuple-element.8), channel_id=1, source_target_pairs={{4,0},{8,4},{12,8},{5,1},{9,5},{13,9},{6,2},{10,6},{14,10},{7,3},{... | collective-permute-start | bytes 1376264 | tf_op jit(solution)/shard_map/ppermute | solution.py:18
  169.8 13.9 %collective-permute-start.4 = (f32[7,16,1024]{2,1,0:T(8,128)S(1)}, f32[7,16,1024]{2,1,0:T(8,128)S(1)}, u32[]{:S(2)}, u32[]{:S(2)}) collective-permute-start(f32[7,16,1024]{2,1,0:T(8,128)S(1)} %get-tuple-element.7), channel_id=1, source_target_pairs={{0,4},{4,8},{8,12},{1,5},{5,9},{9,13},{2,6},{6,10},{10,14},{3,7},{... | collective-permute-start | bytes 1376264 | tf_op jit(solution)/shard_map/ppermute | solution.py:17
  195.9 12.4 %copy-start.2 = (f32[1,24,16,1024]{3,2,1,0:T(8,128)S(1)}, f32[1,24,16,1024]{3,2,1,0:T(8,128)}, u32[]{:S(2)}) copy-start(f32[1,24,16,1024]{3,2,1,0:T(8,128)} %param.3) | copy-start | bytes 4718596
  223.7 13.7 %collective-permute-start.7 = (f32[7,16,1024]{2,1,0:T(8,128)S(1)}, f32[7,16,1024]{2,1,0:T(8,128)S(1)}, u32[]{:S(2)}, u32[]{:S(2)}) collective-permute-start(f32[7,16,1024]{2,1,0:T(8,128)S(1)} %get-tuple-element.6), channel_id=1, source_target_pairs={{4,0},{8,4},{12,8},{5,1},{9,5},{13,9},{6,2},{10,6},{14,10},{7,3},{... | collective-permute-start | bytes 1376264 | tf_op jit(solution)/shard_map/ppermute | solution.py:18
  225.3 13.5 %collective-permute-start.6 = (f32[7,16,1024]{2,1,0:T(8,128)S(1)}, f32[7,16,1024]{2,1,0:T(8,128)S(1)}, u32[]{:S(2)}, u32[]{:S(2)}) collective-permute-start(f32[7,16,1024]{2,1,0:T(8,128)S(1)} %get-tuple-element.5), channel_id=1, source_target_pairs={{0,4},{4,8},{8,12},{1,5},{5,9},{9,13},{2,6},{6,10},{10,14},{3,7},{... | collective-permute-start | bytes 1376264 | tf_op jit(solution)/shard_map/ppermute | solution.py:17
Sparse Core Ops, SparseCore 0:
  121.7 44.9 all-reduce.10
  279.6 44.1 all-reduce.12
where the time goes:
time: 335 us; the launch traced here: 333 us
  other arithmetic  166 us (50%)
  waiting for transfers between devices  125 us (37%)
  starting transfers between devices  24.8 us (7%)
  between operations  13.7 us (4%)
  local copies, waits for them, and re-layouts  4.11 us (1%)
    add x8, other arithmetic, valid_along(): summed + weight * lax.slice_in_dim(padded, offset, offset + length_out, a...  97.8 us
    psum x2, waiting for transfers between devices, local(): log_total = lax.psum(log_terms, 'view')  89.5 us
    log x2, other arithmetic, local(): log_terms = jnp.log(correction)  32.4 us
    div x2, other arithmetic, local(): quotient = recorded[0] / blurred  30.7 us
    ppermute x4, waiting for transfers between devices, with_halo(): after = lax.ppermute(initial, axis, down)  25.9 us
    ppermute x4, starting transfers between devices, with_halo(): before = lax.ppermute(last, axis, up)  19.4 us
    ppermute x4, waiting for transfers between devices, with_halo(): before = lax.ppermute(last, axis, up)  9.9 us
  transfers between devices with their start and end apart: 10, of which 10 were waited for; matrix products, arithmetic and copies ran while one was open for 1% of the time, Pallas kernels for 0%

commit v1 on v0

--- a/solution.py
+++ b/solution.py
@@ -58,7 +58,13 @@
             valid_along(quotient_wide, kernel_view[0], 0, True), kernel_view, True
         )
         log_terms = jnp.log(correction)
-        log_total = lax.psum(log_terms, "view")
+        size = lax.axis_size("view")
+        log_total, far = (log_terms, 1)
+        while far < size:
+            log_total = log_total + lax.ppermute(
+                log_total, "view", [(i_2, i_2 ^ far) for i_2 in range(size)]
+            )
+            far = 2 * far
         estimate = estimate * jnp.exp(log_total / view_total)
     return estimate
 

time: 335 us -> 339 us (1.012)
  other arithmetic: 166 us -> 192 us
  between operations: 13.7 us -> 0.29 us
  waiting for transfers between devices: 125 us -> 112 us
  starting transfers between devices: 24.8 us -> 28.7 us
    psum x2 -> x0, waiting for transfers between devices: 89.5 us -> none  [local(): log_total = lax.psum(log_terms, 'view')]
    ppermute x0 -> x4, waiting for transfers between devices: none -> 76.7 us  [local(): lax.ppermute(log_total, 'view', [(i_2, i_2 ^ far) for i_2 in range(size)])]
    add x0 -> x2, other arithmetic: none -> 30.1 us  [local(): log_total + lax.ppermute(log_total, 'view', [(i_2, i_2 ^ far) for i_2 in...]
  transfers between devices with their start and end apart: 10 -> 12, of which waited for: 10 -> 12; matrix products, arithmetic and copies ran while one was open for 1% -> 1% of each run, Pallas kernels for 0% -> 0%
where the time goes in v1:
time: 339 us; the launch traced here: 337 us
  other arithmetic  192 us (57%)
  waiting for transfers between devices  112 us (33%)
  starting transfers between devices  28.7 us (8%)
  local copies, waits for them, and re-layouts  4.23 us (1%)
    add x8, other arithmetic, valid_along(): summed + weight * lax.slice_in_dim(padded, offset, offset + length_out, a...  99.5 us
    ppermute x4, waiting for transfers between devices, local(): lax.ppermute(log_total, 'view', [(i_2, i_2 ^ far) for i_2 in range(size)])  76.7 us
    div x2, other arithmetic, local(): quotient = recorded[0] / blurred  30.1 us
    log x2, other arithmetic, local(): log_terms = jnp.log(correction)  30.1 us
    add x2, other arithmetic, local(): log_total + lax.ppermute(log_total, 'view', [(i_2, i_2 ^ far) for i_2 in...  30.1 us
    ppermute x4, waiting for transfers between devices, with_halo(): after = lax.ppermute(initial, axis, down)  25.3 us
    ppermute x4, starting transfers between devices, with_halo(): before = lax.ppermute(last, axis, up)  20.3 us
    ppermute x4, waiting for transfers between devices, with_halo(): before = lax.ppermute(last, axis, up)  9.63 us
  transfers between devices with their start and end apart: 12, of which 12 were waited for; matrix products, arithmetic and copies ran while one was open for 1% of the time, Pallas kernels for 0%

profile of v1, /device:TPU:0, one launch (start us, length us, event | category | flops | bytes accessed | tf_op | source)
XLA Modules:
  0.0 336.9 jit_solution(16275903649097213465)
XLA Ops:
  0.0 1.3 fusion.365
  1.4 5.0 %collective-permute-start = (f32[7,16,1024]{2,1,0:T(8,128)S(1)}, f32[7,16,1024]{2,1,0:T(8,128)S(1)}, u32[]{:S(2)}, u32[]{:S(2)}) collective-permute-start(f32[7,16,1024]{2,1,0:T(8,128)S(1)} %get-tuple-element.13), channel_id=1, source_target_pairs={{0,4},{4,8},{8,12},{1,5},{5,9},{9,13},{2,6},{6,10},{10,14},{3,7},{... | collective-permute-start | bytes 1376264 | tf_op jit(solution)/shard_map/ppermute | solution.py:17
  6.4 1.3 collective-permute-start.1
  10.0 6.1 %collective-permute-done = f32[7,16,1024]{2,1,0:T(8,128)S(1)} collective-permute-done((f32[7,16,1024]{2,1,0:T(8,128)S(1)}, f32[7,16,1024]{2,1,0:T(8,128)S(1)}, u32[]{:S(2)}, u32[]{:S(2)}) %collective-permute-start) | collective-permute-done | bytes 458784 | tf_op jit(solution)/shard_map/ppermute | solution.py:17
  16.6 3.7 %collective-permute-done.1 = f32[7,16,1024]{2,1,0:T(8,128)S(1)} collective-permute-done((f32[7,16,1024]{2,1,0:T(8,128)S(1)}, f32[7,16,1024]{2,1,0:T(8,128)S(1)}, u32[]{:S(2)}, u32[]{:S(2)}) %collective-permute-start.1) | collective-permute-done | bytes 458784 | tf_op jit(solution)/shard_map/ppermute | solution.py:18
  20.3 12.4 %fusion.346 = f32[24,16,1024]{2,1,0:T(8,128)S(1)} fusion(f32[31,16,1024]{2,1,0:T(8,128)S(1)} %constant_dynamic-update-slice_fusion.2, f32[31,16,1024]{2,1,0:T(8,128)S(1)} %get-tuple-element.11, f32[24,16,1024]{2,1,0:T(8,128)S(1)} %copy-done, f32[]{:T(128)} %bitcast.19, f32[]{:T(128)} %bitcast.18, f32[]{:T(128)} %bitcast.17, f32[]{:T(128)} %bitcast.16, ...), kind=kLoop, calls=%fused_computation.537 | loop fusion | flops 11403264 | bytes 25165884 | tf_op jit(solution)/shard_map/add | solution.py:30
  32.7 12.4 %fusion.242 = f32[24,16,1024]{2,1,0:T(8,128)S(1)} fusion(f32[24,16,1024]{2,1,0:T(8,128)S(1)} %fusion.346, f32[]{:T(128)} %bitcast.32, f32[]{:T(128)} %bitcast.31, f32[]{:T(128)} %bitcast.30, f32[]{:T(128)} %bitcast.29, f32[]{:T(128)} %bitcast.28, f32[]{:T(128)} %bitcast.27, f32[]{:T(128)} %bitcast.26, f32[]{:T(128)} %bitcast.25, f32[]{:T(128)} %bitcast.24, ...), kind=kLoop, calls=%fused_computation.426 | loop fusion | flops 11403264 | bytes 3145788 | tf_op jit(solution)/shard_map/add | solution.py:30
  45.1 15.0 %fusion.15 = f32[24,16,1024]{2,1,0:T(8,128)S(1)} fusion(f32[24,16,1024]{2,1,0:T(8,128)S(1)} %fusion.242, f32[1,24,16,1024]{3,2,1,0:T(8,128)S(1)} %copy-done.1, f32[]{:T(128)} %bitcast.45, f32[]{:T(128)} %bitcast.44, f32[]{:T(128)} %bitcast.43, f32[]{:T(128)} %bitcast.42, f32[]{:T(128)} %bitcast.41, f32[]{:T(128)} %bitcast.40, f32[]{:T(128)} %bitcast.39, ...), kind=kLoop, calls=%fused_computation.199 | loop fusion | flops 11796480 | bytes 4718652 | tf_op jit(solution)/shard_map/div | solution.py:55
  61.5 4.8 %collective-permute-start.2 = (f32[7,16,1024]{2,1,0:T(8,128)S(1)}, f32[7,16,1024]{2,1,0:T(8,128)S(1)}, u32[]{:S(2)}, u32[]{:S(2)}) collective-permute-start(f32[7,16,1024]{2,1,0:T(8,128)S(1)} %get-tuple-element.9), channel_id=1, source_target_pairs={{0,4},{4,8},{8,12},{1,5},{5,9},{9,13},{2,6},{6,10},{10,14},{3,7},{... | collective-permute-start | bytes 1376264 | tf_op jit(solution)/shard_map/ppermute | solution.py:17
  66.3 7.0 %collective-permute-done.3 = f32[7,16,1024]{2,1,0:T(8,128)S(1)} collective-permute-done((f32[7,16,1024]{2,1,0:T(8,128)S(1)}, f32[7,16,1024]{2,1,0:T(8,128)S(1)}, u32[]{:S(2)}, u32[]{:S(2)}) %collective-permute-start.3) | collective-permute-done | bytes 458784 | tf_op jit(solution)/shard_map/ppermute | solution.py:18
  74.4 12.6 %fusion.193 = f32[24,16,1024]{2,1,0:T(8,128)S(1)} fusion(f32[24,16,1024]{2,1,0:T(8,128)S(1)} %fusion.15, f32[7,16,1024]{2,1,0:T(8,128)S(1)} %collective-permute-done.3, f32[7,16,1024]{2,1,0:T(8,128)S(1)} %collective-permute-done.2, f32[]{:T(128)} %bitcast.19, f32[]{:T(128)} %bitcast.18, f32[]{:T(128)} %bitcast.17, f32[]{:T(128)} %bitcast.16, f32[]{:T(128)} %bitcast.15, ...), kind=kLoop, calls=%fused_computation.377 | loop fusion | flops 16908288 | bytes 4063292 | tf_op jit(solution)/shard_map/add | solution.py:30
  87.0 12.3 %fusion.270 = f32[24,16,1024]{2,1,0:T(8,128)S(1)} fusion(f32[24,16,1024]{2,1,0:T(8,128)S(1)} %fusion.193, f32[]{:T(128)} %bitcast.32, f32[]{:T(128)} %bitcast.31, f32[]{:T(128)} %bitcast.30, f32[]{:T(128)} %bitcast.29, f32[]{:T(128)} %bitcast.28, f32[]{:T(128)} %bitcast.27, f32[]{:T(128)} %bitcast.26, f32[]{:T(128)} %bitcast.25, f32[]{:T(128)} %bitcast.24, ...), kind=kLoop, calls=%fused_computation.454 | loop fusion | flops 11403264 | bytes 3145788 | tf_op jit(solution)/shard_map/add | solution.py:30
  99.4 15.0 %fusion.361 = f32[24,16,1024]{2,1,0:T(8,128)S(1)} fusion(f32[24,16,1024]{2,1,0:T(8,128)S(1)} %fusion.270, f32[]{:T(128)} %bitcast.45, f32[]{:T(128)} %bitcast.44, f32[]{:T(128)} %bitcast.43, f32[]{:T(128)} %bitcast.42, f32[]{:T(128)} %bitcast.41, f32[]{:T(128)} %bitcast.40, f32[]{:T(128)} %bitcast.39, f32[]{:T(128)} %bitcast.38, f32[]{:T(128)} %bitcast.37, ...), kind=kLoop, calls=%fused_computation.567 | loop fusion | flops 11403264 | bytes 3145788 | tf_op jit(solution)/shard_map/log | solution.py:60
  114.5 3.4 %collective-permute-done.4 = f32[24,16,1024]{2,1,0:T(8,128)S(1)} collective-permute-done((f32[24,16,1024]{2,1,0:T(8,128)S(1)}, f32[24,16,1024]{2,1,0:T(8,128)S(1)}, u32[]{:S(2)}, u32[]{:S(2)}) %collective-permute-start.4) | collective-permute-done | bytes 1572896 | tf_op jit(solution)/shard_map/ppermute | solution.py:64
  117.9 15.0 %fusion.370 = f32[24,16,1024]{2,1,0:T(8,128)S(1)} fusion(f32[24,16,1024]{2,1,0:T(8,128)S(1)} %collective-permute-done.4, f32[]{:T(128)} %bitcast.4, f32[]{:T(128)} %bitcast.33, f32[]{:T(128)} %bitcast.34, f32[]{:T(128)} %bitcast.35, f32[]{:T(128)} %bitcast.36, f32[]{:T(128)} %bitcast.37, f32[]{:T(128)} %bitcast.38, f32[24,16,1024]{2,1,0:T(8,128)S(1)} %fusion.270, ...), kind=kLoop, calls=%fused_computation.581 | loop fusion | flops 11796480 | bytes 4718652 | tf_op jit(solution)/shard_map/add | solution.py:64
  132.9 1.6 collective-permute-start.5
  134.5 34.9 %collective-permute-done.5 = f32[24,16,1024]{2,1,0:T(8,128)S(1)} collective-permute-done((f32[24,16,1024]{2,1,0:T(8,128)S(1)}, f32[24,16,1024]{2,1,0:T(8,128)S(1)}, u32[]{:S(2)}, u32[]{:S(2)}) %collective-permute-start.5) | collective-permute-done | bytes 1572896 | tf_op jit(solution)/shard_map/ppermute | solution.py:64
  171.3 5.3 %collective-permute-start.6 = (f32[7,16,1024]{2,1,0:T(8,128)S(1)}, f32[7,16,1024]{2,1,0:T(8,128)S(1)}, u32[]{:S(2)}, u32[]{:S(2)}) collective-permute-start(f32[7,16,1024]{2,1,0:T(8,128)S(1)} %get-tuple-element.7), channel_id=1, source_target_pairs={{0,4},{4,8},{8,12},{1,5},{5,9},{9,13},{2,6},{6,10},{10,14},{3,7},{... | collective-permute-start | bytes 1376264 | tf_op jit(solution)/shard_map/ppermute | solution.py:17
  176.6 7.8 %collective-permute-done.7 = f32[7,16,1024]{2,1,0:T(8,128)S(1)} collective-permute-done((f32[7,16,1024]{2,1,0:T(8,128)S(1)}, f32[7,16,1024]{2,1,0:T(8,128)S(1)}, u32[]{:S(2)}, u32[]{:S(2)}) %collective-permute-start.7) | collective-permute-done | bytes 458784 | tf_op jit(solution)/shard_map/ppermute | solution.py:18
  185.5 12.6 %fusion.155 = f32[24,16,1024]{2,1,0:T(8,128)S(1)} fusion(f32[24,16,1024]{2,1,0:T(8,128)S(1)} %exponential_multiply_fusion.1, f32[7,16,1024]{2,1,0:T(8,128)S(1)} %collective-permute-done.7, f32[7,16,1024]{2,1,0:T(8,128)S(1)} %collective-permute-done.6, f32[]{:T(128)} %bitcast.19, f32[]{:T(128)} %bitcast.18, f32[]{:T(128)} %bitcast.17, f32[]{:T(128)} %bitcast.16, ...), kind=kLoop, calls=%fused_computation.339 | loop fusion | flops 16908288 | bytes 4063292 | tf_op jit(solution)/shard_map/add | solution.py:30
  198.1 12.3 %fusion.298 = f32[24,16,1024]{2,1,0:T(8,128)S(1)} fusion(f32[24,16,1024]{2,1,0:T(8,128)S(1)} %fusion.155, f32[]{:T(128)} %bitcast.32, f32[]{:T(128)} %bitcast.31, f32[]{:T(128)} %bitcast.30, f32[]{:T(128)} %bitcast.29, f32[]{:T(128)} %bitcast.28, f32[]{:T(128)} %bitcast.27, f32[]{:T(128)} %bitcast.26, f32[]{:T(128)} %bitcast.25, f32[]{:T(128)} %bitcast.24, ...), kind=kLoop, calls=%fused_computation.482 | loop fusion | flops 11403264 | bytes 3145788 | tf_op jit(solution)/shard_map/add | solution.py:30
  210.5 15.0 %fusion.72 = f32[24,16,1024]{2,1,0:T(8,128)S(1)} fusion(f32[24,16,1024]{2,1,0:T(8,128)S(1)} %fusion.298, f32[1,24,16,1024]{3,2,1,0:T(8,128)S(1)} %copy-done.1, f32[]{:T(128)} %bitcast.45, f32[]{:T(128)} %bitcast.44, f32[]{:T(128)} %bitcast.43, f32[]{:T(128)} %bitcast.42, f32[]{:T(128)} %bitcast.41, f32[]{:T(128)} %bitcast.40, f32[]{:T(128)} %bitcast.39, ...), kind=kLoop, calls=%fused_computation.256 | loop fusion | flops 11796480 | bytes 4718652 | tf_op jit(solution)/shard_map/div | solution.py:55
  226.9 5.3 %collective-permute-start.8 = (f32[7,16,1024]{2,1,0:T(8,128)S(1)}, f32[7,16,1024]{2,1,0:T(8,128)S(1)}, u32[]{:S(2)}, u32[]{:S(2)}) collective-permute-start(f32[7,16,1024]{2,1,0:T(8,128)S(1)} %get-tuple-element.5), channel_id=1, source_target_pairs={{0,4},{4,8},{8,12},{1,5},{5,9},{9,13},{2,6},{6,10},{10,14},{3,7},{... | collective-permute-start | bytes 1376264 | tf_op jit(solution)/shard_map/ppermute | solution.py:17
  232.2 6.9 %collective-permute-done.9 = f32[7,16,1024]{2,1,0:T(8,128)S(1)} collective-permute-done((f32[7,16,1024]{2,1,0:T(8,128)S(1)}, f32[7,16,1024]{2,1,0:T(8,128)S(1)}, u32[]{:S(2)}, u32[]{:S(2)}) %collective-permute-start.9) | collective-permute-done | bytes 458784 | tf_op jit(solution)/shard_map/ppermute | solution.py:18
  240.2 12.6 %fusion.117 = f32[24,16,1024]{2,1,0:T(8,128)S(1)} fusion(f32[24,16,1024]{2,1,0:T(8,128)S(1)} %fusion.72, f32[7,16,1024]{2,1,0:T(8,128)S(1)} %collective-permute-done.9, f32[7,16,1024]{2,1,0:T(8,128)S(1)} %collective-permute-done.8, f32[]{:T(128)} %bitcast.19, f32[]{:T(128)} %bitcast.18, f32[]{:T(128)} %bitcast.17, f32[]{:T(128)} %bitcast.16, f32[]{:T(128)} %bitcast.15, ...), kind=kLoop, calls=%fused_computation.301 | loop fusion | flops 16908288 | bytes 4063292 | tf_op jit(solution)/shard_map/add | solution.py:30
  252.9 12.3 %fusion.326 = f32[24,16,1024]{2,1,0:T(8,128)S(1)} fusion(f32[24,16,1024]{2,1,0:T(8,128)S(1)} %fusion.117, f32[]{:T(128)} %bitcast.32, f32[]{:T(128)} %bitcast.31, f32[]{:T(128)} %bitcast.30, f32[]{:T(128)} %bitcast.29, f32[]{:T(128)} %bitcast.28, f32[]{:T(128)} %bitcast.27, f32[]{:T(128)} %bitcast.26, f32[]{:T(128)} %bitcast.25, f32[]{:T(128)} %bitcast.24, ...), kind=kLoop, calls=%fused_computation.510 | loop fusion | flops 11403264 | bytes 3145788 | tf_op jit(solution)/shard_map/add | solution.py:30
  265.2 15.0 %fusion.360 = f32[24,16,1024]{2,1,0:T(8,128)S(1)} fusion(f32[24,16,1024]{2,1,0:T(8,128)S(1)} %fusion.326, f32[]{:T(128)} %bitcast.45, f32[]{:T(128)} %bitcast.44, f32[]{:T(128)} %bitcast.43, f32[]{:T(128)} %bitcast.42, f32[]{:T(128)} %bitcast.41, f32[]{:T(128)} %bitcast.40, f32[]{:T(128)} %bitcast.39, f32[]{:T(128)} %bitcast.38, f32[]{:T(128)} %bitcast.37, ...), kind=kLoop, calls=%fused_computation.566 | loop fusion | flops 11403264 | bytes 3145788 | tf_op jit(solution)/shard_map/log | solution.py:60
  280.3 3.4 %collective-permute-done.10 = f32[24,16,1024]{2,1,0:T(8,128)S(1)} collective-permute-done((f32[24,16,1024]{2,1,0:T(8,128)S(1)}, f32[24,16,1024]{2,1,0:T(8,128)S(1)}, u32[]{:S(2)}, u32[]{:S(2)}) %collective-permute-start.10) | collective-permute-done | bytes 1572896 | tf_op jit(solution)/shard_map/ppermute | solution.py:64
  283.7 15.0 %fusion.369 = f32[24,16,1024]{2,1,0:T(8,128)S(1)} fusion(f32[24,16,1024]{2,1,0:T(8,128)S(1)} %collective-permute-done.10, f32[]{:T(128)} %bitcast.4, f32[]{:T(128)} %bitcast.33, f32[]{:T(128)} %bitcast.34, f32[]{:T(128)} %bitcast.35, f32[]{:T(128)} %bitcast.36, f32[]{:T(128)} %bitcast.37, f32[]{:T(128)} %bitcast.38, f32[24,16,1024]{2,1,0:T(8,128)S(1)} %fusion.326, ...), kind=kLoop, calls=%fused_computation.580 | loop fusion | flops 11796480 | bytes 4718652 | tf_op jit(solution)/shard_map/add | solution.py:64
  298.7 1.6 collective-permute-start.11
  300.3 34.9 %collective-permute-done.11 = f32[24,16,1024]{2,1,0:T(8,128)S(1)} collective-permute-done((f32[24,16,1024]{2,1,0:T(8,128)S(1)}, f32[24,16,1024]{2,1,0:T(8,128)S(1)}, u32[]{:S(2)}, u32[]{:S(2)}) %collective-permute-start.11) | collective-permute-done | bytes 1572896 | tf_op jit(solution)/shard_map/ppermute | solution.py:64
  335.2 1.6 exponential_multiply_fusion
  (26 shorter events, 11.1 us)
Async XLA Ops:
  0.0 16.1 %copy-start = (f32[24,16,1024]{2,1,0:T(8,128)S(1)}, f32[24,16,1024]{2,1,0:T(8,128)}, u32[]{:S(2)}) copy-start(f32[24,16,1024]{2,1,0:T(8,128)} %param.5) | copy-start | bytes 4718596
  0.0 7.7 %copy-start.2 = (f32[1,3,15]{2,0,1:T(1,128)S(1)}, f32[1,3,15]{2,0,1:T(1,128)}, u32[]{:S(2)}) copy-start(f32[1,3,15]{2,0,1:T(1,128)} %param.4) | copy-start | bytes 544
  1.4 14.7 %collective-permute-start = (f32[7,16,1024]{2,1,0:T(8,128)S(1)}, f32[7,16,1024]{2,1,0:T(8,128)S(1)}, u32[]{:S(2)}, u32[]{:S(2)}) collective-permute-start(f32[7,16,1024]{2,1,0:T(8,128)S(1)} %get-tuple-element.13), channel_id=1, source_target_pairs={{0,4},{4,8},{8,12},{1,5},{5,9},{9,13},{2,6},{6,10},{10,14},{3,7},{... | collective-permute-start | bytes 1376264 | tf_op jit(solution)/shard_map/ppermute | solution.py:17
  6.4 13.9 %collective-permute-start.1 = (f32[7,16,1024]{2,1,0:T(8,128)S(1)}, f32[7,16,1024]{2,1,0:T(8,128)S(1)}, u32[]{:S(2)}, u32[]{:S(2)}) collective-permute-start(f32[7,16,1024]{2,1,0:T(8,128)S(1)} %get-tuple-element.14), channel_id=1, source_target_pairs={{4,0},{8,4},{12,8},{5,1},{9,5},{13,9},{6,2},{10,6},{14,10},{7,3},{... | collective-permute-start | bytes 1376264 | tf_op jit(solution)/shard_map/ppermute | solution.py:18
  32.6 12.4 %copy-start.1 = (f32[1,24,16,1024]{3,2,1,0:T(8,128)S(1)}, f32[1,24,16,1024]{3,2,1,0:T(8,128)}, u32[]{:S(2)}) copy-start(f32[1,24,16,1024]{3,2,1,0:T(8,128)} %param.3) | copy-start | bytes 4718596
  60.2 13.0 %collective-permute-start.3 = (f32[7,16,1024]{2,1,0:T(8,128)S(1)}, f32[7,16,1024]{2,1,0:T(8,128)S(1)}, u32[]{:S(2)}, u32[]{:S(2)}) collective-permute-start(f32[7,16,1024]{2,1,0:T(8,128)S(1)} %get-tuple-element.10), channel_id=1, source_target_pairs={{4,0},{8,4},{12,8},{5,1},{9,5},{13,9},{6,2},{10,6},{14,10},{7,3},{... | collective-permute-start | bytes 1376264 | tf_op jit(solution)/shard_map/ppermute | solution.py:18
  61.5 12.9 %collective-permute-start.2 = (f32[7,16,1024]{2,1,0:T(8,128)S(1)}, f32[7,16,1024]{2,1,0:T(8,128)S(1)}, u32[]{:S(2)}, u32[]{:S(2)}) collective-permute-start(f32[7,16,1024]{2,1,0:T(8,128)S(1)} %get-tuple-element.9), channel_id=1, source_target_pairs={{0,4},{4,8},{8,12},{1,5},{5,9},{9,13},{2,6},{6,10},{10,14},{3,7},{... | collective-permute-start | bytes 1376264 | tf_op jit(solution)/shard_map/ppermute | solution.py:17
  114.4 3.5 %collective-permute-start.4 = (f32[24,16,1024]{2,1,0:T(8,128)S(1)}, f32[24,16,1024]{2,1,0:T(8,128)S(1)}, u32[]{:S(2)}, u32[]{:S(2)}) collective-permute-start(f32[24,16,1024]{2,1,0:T(8,128)S(1)} %fusion.361), channel_id=1, source_target_pairs={{0,1},{1,0},{2,3},{3,2},{4,5},{5,4},{6,7},{7,6},{8,9},{9,8},{10,11... | collective-permute-start | bytes 4718600 | tf_op jit(solution)/shard_map/ppermute | solution.py:64
  132.9 36.5 %collective-permute-start.5 = (f32[24,16,1024]{2,1,0:T(8,128)S(1)}, f32[24,16,1024]{2,1,0:T(8,128)S(1)}, u32[]{:S(2)}, u32[]{:S(2)}) collective-permute-start(f32[24,16,1024]{2,1,0:T(8,128)S(1)} %fusion.370), channel_id=1, source_target_pairs={{0,2},{1,3},{2,0},{3,1},{4,6},{5,7},{6,4},{7,5},{8,10},{9,11},{10,... | collective-permute-start | bytes 4718600 | tf_op jit(solution)/shard_map/ppermute | solution.py:64
  170.0 14.3 %collective-permute-start.7 = (f32[7,16,1024]{2,1,0:T(8,128)S(1)}, f32[7,16,1024]{2,1,0:T(8,128)S(1)}, u32[]{:S(2)}, u32[]{:S(2)}) collective-permute-start(f32[7,16,1024]{2,1,0:T(8,128)S(1)} %get-tuple-element.8), channel_id=1, source_target_pairs={{4,0},{8,4},{12,8},{5,1},{9,5},{13,9},{6,2},{10,6},{14,10},{7,3},{... | collective-permute-start | bytes 1376264 | tf_op jit(solution)/shard_map/ppermute | solution.py:18
  171.3 14.2 %collective-permute-start.6 = (f32[7,16,1024]{2,1,0:T(8,128)S(1)}, f32[7,16,1024]{2,1,0:T(8,128)S(1)}, u32[]{:S(2)}, u32[]{:S(2)}) collective-permute-start(f32[7,16,1024]{2,1,0:T(8,128)S(1)} %get-tuple-element.7), channel_id=1, source_target_pairs={{0,4},{4,8},{8,12},{1,5},{5,9},{9,13},{2,6},{6,10},{10,14},{3,7},{... | collective-permute-start | bytes 1376264 | tf_op jit(solution)/shard_map/ppermute | solution.py:17
  225.6 13.5 %collective-permute-start.9 = (f32[7,16,1024]{2,1,0:T(8,128)S(1)}, f32[7,16,1024]{2,1,0:T(8,128)S(1)}, u32[]{:S(2)}, u32[]{:S(2)}) collective-permute-start(f32[7,16,1024]{2,1,0:T(8,128)S(1)} %get-tuple-element.6), channel_id=1, source_target_pairs={{4,0},{8,4},{12,8},{5,1},{9,5},{13,9},{6,2},{10,6},{14,10},{7,3},{... | collective-permute-start | bytes 1376264 | tf_op jit(solution)/shard_map/ppermute | solution.py:18
  226.9 13.4 %collective-permute-start.8 = (f32[7,16,1024]{2,1,0:T(8,128)S(1)}, f32[7,16,1024]{2,1,0:T(8,128)S(1)}, u32[]{:S(2)}, u32[]{:S(2)}) collective-permute-start(f32[7,16,1024]{2,1,0:T(8,128)S(1)} %get-tuple-element.5), channel_id=1, source_target_pairs={{0,4},{4,8},{8,12},{1,5},{5,9},{9,13},{2,6},{6,10},{10,14},{3,7},{... | collective-permute-start | bytes 1376264 | tf_op jit(solution)/shard_map/ppermute | solution.py:17
  280.2 3.5 %collective-permute-start.10 = (f32[24,16,1024]{2,1,0:T(8,128)S(1)}, f32[24,16,1024]{2,1,0:T(8,128)S(1)}, u32[]{:S(2)}, u32[]{:S(2)}) collective-permute-start(f32[24,16,1024]{2,1,0:T(8,128)S(1)} %fusion.360), channel_id=1, source_target_pairs={{0,1},{1,0},{2,3},{3,2},{4,5},{5,4},{6,7},{7,6},{8,9},{9,8},{10,11... | collective-permute-start | bytes 4718600 | tf_op jit(solution)/shard_map/ppermute | solution.py:64
  298.7 36.5 %collective-permute-start.11 = (f32[24,16,1024]{2,1,0:T(8,128)S(1)}, f32[24,16,1024]{2,1,0:T(8,128)S(1)}, u32[]{:S(2)}, u32[]{:S(2)}) collective-permute-start(f32[24,16,1024]{2,1,0:T(8,128)S(1)} %fusion.369), channel_id=1, source_target_pairs={{0,2},{1,3},{2,0},{3,1},{4,6},{5,7},{6,4},{7,5},{8,10},{9,11},{10,... | collective-permute-start | bytes 4718600 | tf_op jit(solution)/shard_map/ppermute | solution.py:64
